TPU v7x, 32 devices: a whole 2x2x4 slice. The times are simulated.
32 devices in a mesh: dp: 16 (over z, y, x), tensor: 2 (over core).
Axes of the slice: x: 2, y: 2, z: 4, core: 2. Of those that a mesh axis runs over, the one named last changes fastest.
Arguments:
- images: bfloat16 [64, 256, 768], P(('dp', 'tensor')), may hold values from -6 to 6
- valid_count: int32 [64], P('dp'), may hold values from 16 to 256, as said below
- ln_gain: float32 [2, 2, 768], replicated, may hold values from 0.25 to 1.75
- ln_bias: float32 [2, 2, 768], replicated, may hold values from -1.5 to 1.5
- w_qkv: bfloat16 [2, 768, 3, 768], P(None, None, None, 'tensor'), may hold values from -0.21875 to 0.21875
- qv_bias: float32 [2, 2, 768], P(None, None, 'tensor'), may hold values from -2.5 to 2.5
- w_out: bfloat16 [2, 768, 768], P(None, 'tensor'), may hold values from -0.875 to 0.875
- out_bias: float32 [2, 2, 768], replicated, may hold values from -1.5 to 1.5
- w_up: bfloat16 [2, 768, 3072], P(None, None, 'tensor'), may hold values from -0.21875 to 0.21875
- up_bias: float32 [2, 3072], P(None, 'tensor'), may hold values from -1.5 to 1.5
- w_down: bfloat16 [2, 3072, 768], P(None, 'tensor'), may hold values from -0.109375 to 0.109375
- cotangent: bfloat16 [64, 256, 768], P(('dp', 'tensor')), may hold values from -6 to 6
Outputs:
- layer_out: float32 [64, 256, 768], P(('dp', 'tensor'))
- pooled: float32 [64, 768], P(('dp', 'tensor'))
- input_grad: float32 [64, 256, 768], P(('dp', 'tensor'))
- ln_gain_grad: float32 [2, 2, 768], replicated
- ln_bias_grad: float32 [2, 2, 768], replicated
- qkv_grad: float32 [2, 768, 3, 768], P(None, 'dp', None, 'tensor')
- qv_bias_grad: float32 [2, 2, 768], P(None, None, 'tensor')
- out_grad: float32 [2, 768, 768], P(None, 'tensor', 'dp')
- out_bias_grad: float32 [2, 2, 768], replicated
- up_grad: float32 [2, 768, 3072], P(None, 'dp', 'tensor')
- up_bias_grad: float32 [2, 3072], P(None, 'tensor')
- down_grad: float32 [2, 3072, 768], P(None, 'tensor', 'dp')
Inputs may be any that keep to these rules, and one draw needn't show every extreme that they name: `valid_count`: some image has exactly 256 valid patches and some other exactly 16; an image's valid patches are its first slots.
All inputs are finite; a program needn't handle non-finite values.
Results may differ from a plain program's by a relative error of at most 0.024.
Values may be sent and summed in bfloat16 or wider, within the bound.
No kernel may reach another device: no remote copies, remote signals or barrier semaphores. Data moves between devices by JAX's collectives and lax.ppermute only.
A program may use at most 192 MiB of HBM per device.

v0:
```python
import jax
import jax.numpy as jnp
from jax import lax
from jax.sharding import PartitionSpec as P

HEAD_DIM = 64
LAYERS = 2
EPSILON = 1e-06
NEGATIVE = -1e30


def normalize(values, norm_gain, norm_bias):
    average = jnp.mean(values, axis=-1, keepdims=True)
    centred = values - average
    variance = jnp.mean(centred * centred, axis=-1, keepdims=True)
    return centred * lax.rsqrt(variance + EPSILON) * norm_gain + norm_bias


def gelu_exact(values):
    return jax.nn.gelu(values, approximate=False)


def spread_rows(values):
    return lax.all_gather(values, "tensor", axis=0, tiled=True)


def spread_grads(values):
    return lax.all_gather(values, "tensor", axis=0, tiled=True)


def reduce_branch(left, weight, local_rows):

    def partial_term(start, count):
        return jnp.einsum("isn,nd->isd", left, weight, preferred_element_type=jnp.float32)

    return lax.psum_scatter(
        partial_term(jnp.int32(0), local_rows * lax.axis_size("tensor")).astype(jnp.bfloat16),
        "tensor",
        scatter_dimension=0,
        tiled=True,
    ).astype(jnp.float32)


def reduce_grads(left, weight, local_rows):

    def partial_term(start, count):
        return jnp.einsum("isn,dn->isd", left, weight, preferred_element_type=jnp.float32)

    return lax.psum_scatter(
        partial_term(jnp.int32(0), local_rows * lax.axis_size("tensor")).astype(jnp.bfloat16),
        "tensor",
        scatter_dimension=0,
        tiled=True,
    ).astype(jnp.float32)


def masked_scores(queries, keys_in, key_mask, score_scale):
    scores = (
        jnp.einsum("iqhe,ikhe->ihqk", queries, keys_in, preferred_element_type=jnp.float32)
        * score_scale
    )
    return jnp.where(key_mask[:, None, None, :], scores, NEGATIVE)


def attention_forward(queries, keys_in, values_in, key_mask, score_scale):
    scores = masked_scores(queries, keys_in, key_mask, score_scale)
    largest = jnp.max(scores, axis=-1, keepdims=True)
    exponent = jnp.exp(scores - largest)
    row_total = jnp.sum(exponent, axis=-1, keepdims=True)
    weights = (exponent / row_total).astype(jnp.bfloat16)
    attended = jnp.einsum("ihqk,ikhe->iqhe", weights, values_in, preferred_element_type=jnp.float32)
    return (attended.astype(jnp.bfloat16), largest + jnp.log(row_total))


def attention_backward(queries, keys_in, values_in, key_mask, log_total, grad_out, score_scale):
    scores = masked_scores(queries, keys_in, key_mask, score_scale)
    probs = jnp.exp(scores - log_total)
    grad_probs = jnp.einsum(
        "iqhe,ikhe->ihqk", grad_out, values_in, preferred_element_type=jnp.float32
    )
    grad_values = jnp.einsum(
        "ihqk,iqhe->ikhe", probs.astype(jnp.bfloat16), grad_out, preferred_element_type=jnp.float32
    )
    inner = jnp.sum(grad_probs * probs, axis=-1, keepdims=True)
    grad_scores = (probs * (grad_probs - inner)).astype(jnp.bfloat16)
    grad_queries = (
        jnp.einsum("ihqk,ikhe->iqhe", grad_scores, keys_in, preferred_element_type=jnp.float32)
        * score_scale
    )
    grad_keys = (
        jnp.einsum("ihqk,iqhe->ikhe", grad_scores, queries, preferred_element_type=jnp.float32)
        * score_scale
    )
    return (grad_queries, grad_keys, grad_values)


def shards(
    images,
    valid_count,
    ln_gain,
    ln_bias,
    w_qkv,
    qv_bias,
    w_out,
    out_bias,
    w_up,
    up_bias,
    w_down,
    cotangent,
):
    local_rows = images.shape[0]
    group_rows = valid_count.shape[0]
    slot_count = images.shape[1]
    width = images.shape[2]
    local_width = w_qkv.shape[3]
    head_count = local_width // HEAD_DIM
    score_scale = HEAD_DIM ** (-0.5)
    slot_index = jnp.arange(slot_count, dtype=jnp.int32)
    key_mask = slot_index[None, :] < valid_count[:, None]

    def split_heads(values):
        return values.reshape(group_rows, slot_count, head_count, HEAD_DIM)

    stream = images.astype(jnp.float32)
    saved = []
    for layer_index in range(LAYERS):
        first_in = stream
        first_rows = spread_rows(
            normalize(stream, ln_gain[layer_index, 0], ln_bias[layer_index, 0]).astype(jnp.bfloat16)
        )
        joint = jnp.einsum(
            "isd,dcn->iscn", first_rows, w_qkv[layer_index], preferred_element_type=jnp.float32
        )
        queries = split_heads((joint[:, :, 0] + qv_bias[layer_index, 0]).astype(jnp.bfloat16))
        keys_in = split_heads(joint[:, :, 1].astype(jnp.bfloat16))
        values_in = split_heads((joint[:, :, 2] + qv_bias[layer_index, 1]).astype(jnp.bfloat16))
        attended, log_total = attention_forward(queries, keys_in, values_in, key_mask, score_scale)
        attended = attended.reshape(group_rows, slot_count, local_width)
        stream = stream + (
            reduce_branch(attended, w_out[layer_index], local_rows) + out_bias[layer_index, 0]
        )
        second_in = stream
        second_rows = spread_rows(
            normalize(stream, ln_gain[layer_index, 1], ln_bias[layer_index, 1]).astype(jnp.bfloat16)
        )
        hidden_pre = (
            jnp.einsum(
                "isd,df->isf", second_rows, w_up[layer_index], preferred_element_type=jnp.float32
            )
            + up_bias[layer_index]
        )
        hidden = gelu_exact(hidden_pre).astype(jnp.bfloat16)
        stream = stream + (
            reduce_branch(hidden, w_down[layer_index], local_rows) + out_bias[layer_index, 1]
        )
        saved.append(
            (
                first_in,
                first_rows,
                queries,
                keys_in,
                values_in,
                log_total,
                attended,
                second_in,
                second_rows,
                hidden_pre,
                hidden,
            )
        )
    own_start = lax.axis_index("tensor") * local_rows
    own_counts = lax.dynamic_slice_in_dim(valid_count, own_start, local_rows)
    own_mask = slot_index[None, :] < own_counts[:, None]
    pooled = (
        jnp.sum(jnp.where(own_mask[:, :, None], stream, 0.0), axis=1)
        / own_counts.astype(jnp.float32)[:, None]
    )
    grad_stream = cotangent.astype(jnp.float32)
    weight_parts = [None] * LAYERS
    gain_parts = [None] * LAYERS
    shift_parts = [None] * LAYERS
    outb_parts = [None] * LAYERS
    qv_parts = [None] * LAYERS
    upb_parts = [None] * LAYERS
    for layer_index in reversed(range(LAYERS)):
        (
            first_in,
            first_rows,
            queries,
            keys_in,
            values_in,
            log_total,
            attended,
            second_in,
            second_rows,
            hidden_pre,
            hidden,
        ) = saved[layer_index]
        down_bias_grad = jnp.sum(grad_stream, axis=(0, 1))
        grad_rows = spread_grads(grad_stream.astype(jnp.bfloat16))
        down_grad = jnp.einsum("isf,isd->fd", hidden, grad_rows, preferred_element_type=jnp.float32)
        grad_hidden = jnp.einsum(
            "isd,fd->isf", grad_rows, w_down[layer_index], preferred_element_type=jnp.float32
        )
        grad_pre = jax.vjp(gelu_exact, hidden_pre)[1](grad_hidden)[0]
        hidden_bias_grad = jnp.sum(grad_pre, axis=(0, 1))
        grad_pre_low = grad_pre.astype(jnp.bfloat16)
        up_grad = jnp.einsum(
            "isd,isf->df", second_rows, grad_pre_low, preferred_element_type=jnp.float32
        )
        grad_normed = reduce_grads(grad_pre_low, w_up[layer_index], local_rows)
        grad_in, gain_second, shift_second = jax.vjp(
            normalize, second_in, ln_gain[layer_index, 1], ln_bias[layer_index, 1]
        )[1](grad_normed)
        grad_stream = grad_stream + grad_in
        proj_bias_grad = jnp.sum(grad_stream, axis=(0, 1))
        grad_rows = spread_grads(grad_stream.astype(jnp.bfloat16))
        out_grad = jnp.einsum(
            "isn,isd->nd", attended, grad_rows, preferred_element_type=jnp.float32
        )
        grad_att = jnp.einsum(
            "isd,nd->isn", grad_rows, w_out[layer_index], preferred_element_type=jnp.float32
        )
        grad_att = split_heads(grad_att.astype(jnp.bfloat16))
        grad_queries, grad_keys, grad_values = attention_backward(
            queries, keys_in, values_in, key_mask, log_total, grad_att, score_scale
        )
        grad_queries = grad_queries.reshape(group_rows, slot_count, local_width)
        grad_keys = grad_keys.reshape(group_rows, slot_count, local_width)
        grad_values = grad_values.reshape(group_rows, slot_count, local_width)
        qv_parts[layer_index] = jnp.stack(
            [jnp.sum(grad_queries, axis=(0, 1)), jnp.sum(grad_values, axis=(0, 1))]
        )
        grad_joint = jnp.stack([grad_queries, grad_keys, grad_values], axis=2).astype(jnp.bfloat16)
        qkv_grad = jnp.einsum(
            "isd,iscn->dcn", first_rows, grad_joint, preferred_element_type=jnp.float32
        )
        grad_normed = reduce_grads(
            grad_joint.reshape(group_rows, slot_count, 3 * local_width),
            w_qkv[layer_index].reshape(width, 3 * local_width),
            local_rows,
        )
        grad_in, gain_first, shift_first = jax.vjp(
            normalize, first_in, ln_gain[layer_index, 0], ln_bias[layer_index, 0]
        )[1](grad_normed)
        grad_stream = grad_stream + grad_in
        gain_parts[layer_index] = jnp.stack([gain_first, gain_second])
        shift_parts[layer_index] = jnp.stack([shift_first, shift_second])
        outb_parts[layer_index] = jnp.stack([proj_bias_grad, down_bias_grad])
        upb_parts[layer_index] = hidden_bias_grad
        layer_grads = (qkv_grad, out_grad, up_grad, down_grad)
        weight_parts[layer_index] = layer_grads
    stacked = tuple(
        (
            jnp.stack([weight_parts[layer_index][member] for layer_index in range(LAYERS)])
            for member in range(4)
        )
    )
    summed = (
        lax.psum_scatter(stacked[0], "dp", scatter_dimension=1, tiled=True),
        lax.psum_scatter(stacked[1], "dp", scatter_dimension=2, tiled=True),
        lax.psum_scatter(stacked[2], "dp", scatter_dimension=1, tiled=True),
        lax.psum_scatter(stacked[3], "dp", scatter_dimension=2, tiled=True),
    )
    qv_grads, upb_grads = lax.psum((jnp.stack(qv_parts), jnp.stack(upb_parts)), "dp")
    gain_grads, shift_grads, outb_grads = lax.psum(
        (jnp.stack(gain_parts), jnp.stack(shift_parts), jnp.stack(outb_parts)), ("dp", "tensor")
    )
    return (
        stream,
        pooled,
        grad_stream,
        gain_grads,
        shift_grads,
        summed[0],
        qv_grads,
        summed[1],
        outb_grads,
        summed[2],
        upb_grads,
        summed[3],
    )


def solution(mesh):
    placed = (
        P(("dp", "tensor"), None, None),
        P("dp"),
        P(),
        P(),
        P(None, None, None, "tensor"),
        P(None, None, "tensor"),
        P(None, "tensor", None),
        P(),
        P(None, None, "tensor"),
        P(None, "tensor"),
        P(None, "tensor", None),
        P(("dp", "tensor"), None, None),
    )
    return jax.shard_map(
        shards,
        mesh=mesh,
        in_specs=placed,
        out_specs=(
            P(("dp", "tensor"), None, None),
            P(("dp", "tensor"), None),
            P(("dp", "tensor"), None, None),
            P(),
            P(),
            P(None, "dp", None, "tensor"),
            P(None, None, "tensor"),
            P(None, "tensor", "dp"),
            P(),
            P(None, "dp", "tensor"),
            P(None, "tensor"),
            P(None, "tensor", "dp"),
        ),
        check_vma=False,
    )
```

profile of v0, /device:TPU:0, one launch (start us, length us, event | category | flops | bytes accessed | tf_op | source)
XLA Modules:
  0.0 1126.0 jit_solution(4967242549161505414)
XLA Ops:
  13.7 12.3 %all-gather.9.cloned.1.call-done = bf16[4,256,768]{2,1,0:T(8,128)(2,1)} async-done(((bf16[2,256,768]{2,1,0:T(8,128)(2,1)}), bf16[4,256,768]{2,1,0:T(8,128)(2,1)}) %all-gather.9.cloned.1.call-update) | async-done | bytes 1572880 | tf_op jit(solution)/shard_map/all_gather | solution.py:24
  46.6 10.3 reduce-scatter.11.cloned.1.call-done
  61.7 10.8 all-gather.11.cloned.1.call-done
  72.6 6.3 fusion.95
  78.9 15.5 %multiply_convert_fusion.3 = (bf16[4,256,1536]{2,1,0:T(8,128)(2,1)S(1)}, f32[4,256,1536]{2,1,0:T(8,128)}) fusion(f32[4,256,1536]{2,1,0:T(8,128)S(1)} %get-tuple-element.122, f32[1536]{0:T(1024)S(1)} %get-tuple-element.73, u8[256,1536]{1,0:T(8,128)(4,1)S(1)} %get-tuple-element.51, u8[256,1536]{1,0:T(8,128)(4,1)S(1)} %get-tuple-element.50), kind=kLoop, calls=%fused_computation.40 | loop fusion | flops 111673344 | bytes 16521216 | tf_op jit(solution)/shard_map/convert_element_type | solution.py:152
  96.0 5.3 fusion.65
  101.3 10.3 reduce-scatter.13.cloned.1.call-done
  115.4 10.6 all-gather.13.cloned.1.call-done
  151.5 10.3 reduce-scatter.15.cloned.1.call-done
  166.6 10.2 all-gather.15.cloned.1.call-done
  176.8 6.3 fusion.96
  185.8 15.6 %multiply_convert_fusion.2 = (bf16[4,256,1536]{2,1,0:T(8,128)(2,1)}, f32[4,256,1536]{2,1,0:T(8,128)}) fusion(f32[4,256,1536]{2,1,0:T(8,128)S(1)} %get-tuple-element.125, f32[1536]{0:T(1024)S(1)} %get-tuple-element.72, u8[256,1536]{1,0:T(8,128)(4,1)S(1)} %get-tuple-element.49, u8[256,1536]{1,0:T(8,128)(4,1)S(1)} %get-tuple-element.48), kind=kLoop, calls=%fused_computation.24 | loop fusion | flops 111673344 | bytes 16521216 | tf_op jit(solution)/shard_map/convert_element_type | solution.py:152
  201.4 10.2 fusion.134
  213.3 5.4 fusion.68
  218.7 6.4 fusion.71
  232.3 9.1 reduce-scatter.17.cloned.1.call-done
  263.9 8.0 multiply_reduce_fusion.1
  297.6 5.6 convolution_convert_fusion.3
  303.7 9.9 reduce-scatter.21.cloned.1.call-done
  319.2 11.1 all-gather.21.cloned.1.call-done
  330.3 10.2 fusion.135
  342.3 5.4 fusion.62
  347.8 10.3 reduce-scatter.23.cloned.1.call-done
  366.5 8.7 all-gather.23.cloned.1.call-done
  381.1 5.4 multiply_reduce_fusion
  402.7 5.8 convolution_convert_fusion.2
  423.8 15.1 %copy.141 = f32[2,1536,768]{1,0,2:T(2,128)} copy(f32[2,1536,768]{2,1,0:T(8,128)} %pad_maximum_fusion.1) | data formatting | bytes 18874368 | tf_op jit(solution)/shard_map/stack | solution.py:255
  474.3 81.1 %all-reduce.3 = (f32[2,2,384]{2,1,0:T(2,128)}, f32[2,1536]{1,0:T(2,128)}) all-reduce(f32[2,2,384]{2,1,0:T(2,128)S(1)} %pad_maximum_fusion.10, f32[2,1536]{1,0:T(2,128)S(1)} %pad_maximum_fusion.9), channel_id=1, replica_groups=mesh['dp'=16,'tensor'=2] {'dp'}, use_global_device_ids=true, to_apply=%region_46.47 | all-reduce | flops 4608 | bytes 36864 | tf_op jit(solution)/shard_map/psum | solution.py:265
  559.4 39.5 %all-reduce.2 = (f32[2,2,768]{2,1,0:T(2,128)}, f32[2,2,768]{2,1,0:T(2,128)}, f32[2,2,768]{2,1,0:T(2,128)}) all-reduce(f32[2,2,768]{2,1,0:T(2,128)S(1)} %pad_maximum_fusion.6, f32[2,2,768]{2,1,0:T(2,128)S(1)} %pad_maximum_fusion.7, f32[2,2,768]{2,1,0:T(2,128)S(1)} %pad_maximum_fusion.8), channel_id=1, replica_groups=mesh['dp'=16,'tensor'=2] {'dp','tensor'}, use_global_device_ids=true, to_apply=%region_35.36 | all-reduce | flops 9216 | bytes 73728 | tf_op jit(solution)/shard_map/psum | solution.py:266
  600.6 186.0 %all-reduce.7.cloned.1.call-done = (f32[2,384,768]{1,0,2:T(2,128)}, f32[2,1536,768]{1,0,2:T(2,128)}) async-done(((f32[2,384,768]{1,0,2:T(2,128)}, f32[2,1536,768]{1,0,2:T(2,128)}), (f32[2,384,768]{1,0,2:T(2,128)}, f32[2,1536,768]{1,0,2:T(2,128)})) %all-reduce.7.cloned.1.call-update) | async-done | bytes 11796496
  790.3 173.4 %reduce-scatter.29.cloned.1.call-done = f32[2,48,1536]{2,1,0:T(8,128)} async-done(((f32[2,768,1536]{2,1,0:T(8,128)}), f32[2,48,1536]{2,1,0:T(8,128)}) %reduce-scatter.29.cloned.1.call-update) | async-done | bytes 589840 | tf_op jit(solution)/shard_map/reduce_scatter | solution.py:262
  963.7 155.3 %reduce-scatter.27.cloned.1.call-done = f32[2,48,3,384]{3,1,2,0:T(8,128)} async-done(((f32[2,768,3,384]{3,1,2,0:T(8,128)}), f32[2,48,3,384]{3,1,2,0:T(8,128)}) %reduce-scatter.27.cloned.1.call-update) | async-done | bytes 442384 | tf_op jit(solution)/shard_map/reduce_scatter | solution.py:260
  (347 shorter events, 224.1 us)
Async XLA Ops:
  7.2 18.9 %all-gather.9.cloned.1.call-start = ((), (), s32[]{:S(2)}) async-start(), calls=%async_computation.10 | async-start | bytes 2359296 | tf_op jit(solution)/shard_map/all_gather | solution.py:24
  8.6 21.7 %copy-start.46 = (f32[2,256]{1,0:T(2,128)}, f32[2,256]{1,0:T(2,128)S(1)}, u32[]{:S(2)}) copy-start(f32[2,256]{1,0:T(2,128)S(1)} %broadcast_multiply_fusion.3) | copy-start | bytes 6148
  10.1 20.2 %copy-start.52 = (f32[2,256]{1,0:T(2,128)}, f32[2,256]{1,0:T(2,128)S(1)}, u32[]{:S(2)}) copy-start(f32[2,256]{1,0:T(2,128)S(1)} %fusion.79) | copy-start | bytes 6148
  11.0 19.2 %copy-start.44 = (f32[768]{0:T(1024)}, f32[768]{0:T(1024)S(1)}, u32[]{:S(2)}) copy-start(f32[768]{0:T(1024)S(1)} %get-tuple-element.143) | copy-start | bytes 9220
  13.4 43.5 %reduce-scatter.11.cloned.1.call-start = ((), (), s32[]{:S(2)}) async-start(), calls=%async_computation.11 | async-start | bytes 2359296 | tf_op jit(solution)/shard_map/reduce_scatter | solution.py:36
  13.6 24.4 %copy-start.48 = (f32[6,64]{1,0:T(8,128)}, f32[6,64]{1,0:T(8,128)S(1)}, u32[]{:S(2)}) copy-start(f32[6,64]{1,0:T(8,128)S(1)} %add.272) | copy-start | bytes 4612
  46.5 26.1 %all-gather.11.cloned.1.call-start = ((), (), s32[]{:S(2)}) async-start(), calls=%async_computation.12 | async-start | bytes 2359296 | tf_op jit(solution)/shard_map/all_gather | solution.py:24
  61.4 50.2 %reduce-scatter.13.cloned.1.call-start = ((), (), s32[]{:S(2)}) async-start(), calls=%async_computation.13 | async-start | bytes 2359296 | tf_op jit(solution)/shard_map/reduce_scatter | solution.py:36
  78.9 15.5 %copy-start.26 = (f32[4,256,1536]{2,1,0:T(8,128)}, f32[4,256,1536]{2,1,0:T(8,128)S(1)}, u32[]{:S(2)}) copy-start(f32[4,256,1536]{2,1,0:T(8,128)S(1)} %get-tuple-element.122) | copy-start | bytes 18874372
  101.3 24.7 %all-gather.13.cloned.1.call-start = ((), (), s32[]{:S(2)}) async-start(), calls=%async_computation.14 | async-start | bytes 2359296 | tf_op jit(solution)/shard_map/all_gather | solution.py:24
  114.8 47.0 %reduce-scatter.15.cloned.1.call-start = ((), (), s32[]{:S(2)}) async-start(), calls=%async_computation.15 | async-start | bytes 2359296 | tf_op jit(solution)/shard_map/reduce_scatter | solution.py:36
  151.5 25.3 %all-gather.15.cloned.1.call-start = ((), (), s32[]{:S(2)}) async-start(), calls=%async_computation.16 | async-start | bytes 2359296 | tf_op jit(solution)/shard_map/all_gather | solution.py:24
  165.6 35.8 %all-gather.17.cloned.1.call-start = ((), (), s32[]{:S(2)}) async-start(), calls=%async_computation.18 | async-start | bytes 2359296 | tf_op jit(solution)/shard_map/all_gather | solution.py:28
  166.4 62.7 %reduce-scatter.19.cloned.1.call-start = ((), (), s32[]{:S(2)}) async-start(), calls=%async_computation.19 | async-start | bytes 2359296 | tf_op jit(solution)/shard_map/reduce_scatter | solution.py:49
  218.7 22.8 %reduce-scatter.17.cloned.1.call-start = ((), (), s32[]{:S(2)}) async-start(), calls=%async_computation.17 | async-start | bytes 2359296 | tf_op jit(solution)/shard_map/reduce_scatter | solution.py:36
  225.1 33.1 %all-gather.19.cloned.1.call-start = ((), (), s32[]{:S(2)}) async-start(), calls=%async_computation.20 | async-start | bytes 2359296 | tf_op jit(solution)/shard_map/all_gather | solution.py:28
  247.0 66.6 %reduce-scatter.21.cloned.1.call-start = ((), (), s32[]{:S(2)}) async-start(), calls=%async_computation.21 | async-start | bytes 2359296 | tf_op jit(solution)/shard_map/reduce_scatter | solution.py:49
  303.3 27.1 %all-gather.21.cloned.1.call-start = ((), (), s32[]{:S(2)}) async-start(), calls=%async_computation.22 | async-start | bytes 2359296 | tf_op jit(solution)/shard_map/all_gather | solution.py:28
  319.2 38.9 %reduce-scatter.23.cloned.1.call-start = ((), (), s32[]{:S(2)}) async-start(), calls=%async_computation.23 | async-start | bytes 2359296 | tf_op jit(solution)/shard_map/reduce_scatter | solution.py:49
  347.7 27.5 %all-gather.23.cloned.1.call-start = ((), (), s32[]{:S(2)}) async-start(), calls=%async_computation.24 | async-start | bytes 2359296 | tf_op jit(solution)/shard_map/all_gather | solution.py:28
  364.0 191.3 %reduce-scatter.25.cloned.1.call-start = ((), (), s32[]{:S(2)}) async-start(), calls=%async_computation.25 | async-start | bytes 2359296 | tf_op jit(solution)/shard_map/reduce_scatter | solution.py:49
  408.5 378.1 %all-reduce.7.cloned.1.call-start = ((), (), s32[]{:S(2)}) async-start(), calls=%async_computation.28 | async-start | bytes 23592960
  423.8 15.1 %copy-start.62 = (bf16[4,256,768]{2,1,0:T(8,128)(2,1)S(1)}, bf16[4,256,768]{2,1,0:T(8,128)(2,1)}, u32[]{:S(2)}) copy-start(bf16[4,256,768]{2,1,0:T(8,128)(2,1)} %all-gather.23.cloned.1.call-done) | copy-start | bytes 4718596
  423.8 15.1 %copy-start.66 = (bf16[4,6,64,256]{3,2,1,0:T(8,128)(2,1)S(1)}, bf16[4,6,64,256]{3,2,1,0:T(8,128)(2,1)}, u32[]{:S(2)}) copy-start(bf16[4,6,64,256]{3,2,1,0:T(8,128)(2,1)} %copy-done.65) | copy-start | bytes 2359300
  443.4 520.3 %reduce-scatter.29.cloned.1.call-start = ((), (), s32[]{:S(2)}) async-start(), calls=%async_computation.27 | async-start | bytes 10027008 | tf_op jit(solution)/shard_map/reduce_scatter | solution.py:262
  456.2 662.8 %reduce-scatter.27.cloned.1.call-start = ((), (), s32[]{:S(2)}) async-start(), calls=%async_computation.26 | async-start | bytes 7520256 | tf_op jit(solution)/shard_map/reduce_scatter | solution.py:260
  470.1 85.2 %copy-start.45 = (f32[768]{0:T(1024)S(1)}, f32[768]{0:T(1024)}, u32[]{:S(2)}) copy-start(f32[768]{0:T(1024)} %copy-done.44) | copy-start | bytes 9220
  470.1 85.2 %copy-start.47 = (f32[2,256]{1,0:T(2,128)S(1)}, f32[2,256]{1,0:T(2,128)}, u32[]{:S(2)}) copy-start(f32[2,256]{1,0:T(2,128)} %copy-done.46) | copy-start | bytes 6148
  472.1 85.1 %copy-start.53 = (f32[2,256]{1,0:T(2,128)S(1)}, f32[2,256]{1,0:T(2,128)}, u32[]{:S(2)}) copy-start(f32[2,256]{1,0:T(2,128)} %copy-done.52) | copy-start | bytes 6148
  472.1 85.1 %copy-start.51 = (f32[2,256]{1,0:T(2,128)S(1)}, f32[2,256]{1,0:T(2,128)}, u32[]{:S(2)}) copy-start(f32[2,256]{1,0:T(2,128)} %copy-done.50) | copy-start | bytes 6148
  472.4 126.5 %copy-start.7 = (f32[2,256,768]{2,1,0:T(8,128)S(1)}, f32[2,256,768]{2,1,0:T(8,128)}, u32[]{:S(2)}) copy-start(f32[2,256,768]{2,1,0:T(8,128)} %copy-done.6) | copy-start | bytes 4718596
  555.4 43.6 %copy-start.24 = (bf16[2,256,768]{2,1,0:T(8,128)(2,1)S(1)}, bf16[2,256,768]{2,1,0:T(8,128)(2,1)}, u32[]{:S(2)}) copy-start(bf16[2,256,768]{2,1,0:T(8,128)(2,1)} %reduce-scatter.25.cloned.1.call-done) | copy-start | bytes 2359300
  (61 other events, 215.5 us)
Sparse Core Ops, SparseCore 0:
  13.5 12.4 all-gather.8
  46.6 10.2 reduce-scatter.10
  61.5 10.9 all-gather.10
  101.4 10.1 reduce-scatter.12
  114.9 11.0 all-gather.12
  151.6 10.2 reduce-scatter.14
  165.8 10.9 all-gather.14
  178.4 10.9 all-gather.16
  218.8 10.2 reduce-scatter.18
  231.2 10.2 reduce-scatter.16
  247.2 10.9 all-gather.18
  303.4 10.2 reduce-scatter.20
  319.3 10.9 all-gather.20
  347.8 10.2 reduce-scatter.22
  364.1 11.0 all-gather.22
  408.6 10.2 reduce-scatter.24
  443.5 343.0 all-reduce.6
  793.7 169.9 reduce-scatter.28
  969.6 149.3 reduce-scatter.26
where the time goes:
time: 1140 us; the launch traced here: 1130 us
  waiting for transfers between devices  646 us (57%)
  matrix products  144 us (13%)
  blocking collectives  121 us (11%)
  other arithmetic  99.7 us (9%)
  local copies, waits for them, and re-layouts  96.1 us (8%)
  between operations  16.3 us (1%)
    unnamed x20, waiting for transfers between devices  187 us
    reduce_scatter x1, waiting for transfers between devices, shards(): lax.psum_scatter(stacked[2], 'dp', scatter_dimension=1, tiled=True)  173 us
    reduce_scatter x1, waiting for transfers between devices, shards(): lax.psum_scatter(stacked[0], 'dp', scatter_dimension=1, tiled=True)  155 us
    psum x1, blocking collectives, shards(): lax.psum((jnp.stack(qv_parts), jnp.stack(upb_parts)), 'dp')  81.1 us
    all_gather x4, waiting for transfers between devices, spread_rows(): return lax.all_gather(values, 'tensor', axis=0, tiled=True)  43.9 us
    reduce_scatter x4, waiting for transfers between devices, reduce_branch(): lax.psum_scatter(partial_term(jnp.int32(0), local_rows * lax.axis_size('t...  40.1 us
    psum x1, blocking collectives, shards(): lax.psum((jnp.stack(gain_parts), jnp.stack(shift_parts), jnp.stack(outb_p...  39.5 us
    convert_element_type x2, other arithmetic, shards(): hidden = gelu_exact(hidden_pre).astype(jnp.bfloat16)  31.1 us
  transfers between devices with their start and end apart: 19, of which 17 were waited for; matrix products, arithmetic and copies ran while one was open for 10% of the time, Pallas kernels for 0%

commit v1 on v0

--- a/solution.py
+++ b/solution.py
@@ -7,6 +7,11 @@
 LAYERS = 2
 EPSILON = 1e-06
 NEGATIVE = -1e30
+
+
+def exchange_gather(x, axis, along):
+    sent = jnp.stack([x] * lax.axis_size(axis))
+    return jnp.concatenate(lax.all_to_all(sent, axis, 0, 0), axis=along)
 
 
 def normalize(values, norm_gain, norm_bias):
@@ -21,7 +26,7 @@
 
 
 def spread_rows(values):
-    return lax.all_gather(values, "tensor", axis=0, tiled=True)
+    return exchange_gather(values, "tensor", 0)
 
 
 def spread_grads(values):

time: 1140 us -> 1110 us (0.974)
  waiting for transfers between devices: 646 us -> 602 us
  blocking collectives: 121 us -> 142 us
    all_gather x4 -> x0, waiting for transfers between devices: 43.9 us -> none  [spread_rows(): return lax.all_gather(values, 'tensor', axis=0, tiled=True)]
    all_to_all x0 -> x4, blocking collectives: none -> 21.5 us  [exchange_gather(): return jnp.concatenate(lax.all_to_all(sent, axis, 0, 0), axis=along)]
    unnamed x20 -> x16, waiting for transfers between devices: 187 us -> 186 us
    unnamed x153 -> x171, local copies, waits for them, and re-layouts: 25.3 us -> 25.6 us
  transfers between devices with their start and end apart: 19 -> 15, of which waited for: 17 -> 13; matrix products, arithmetic and copies ran while one was open for 10% -> 11% of each run, Pallas kernels for 0% -> 0%
where the time goes in v1:
time: 1110 us; the launch traced here: 1100 us
  waiting for transfers between devices  602 us (54%)
  blocking collectives  142 us (13%)
  matrix products  136 us (12%)
  other arithmetic  102 us (9%)
  local copies, waits for them, and re-layouts  102 us (9%)
  between operations  16.3 us (1%)
    unnamed x16, waiting for transfers between devices  186 us
    reduce_scatter x1, waiting for transfers between devices, shards(): lax.psum_scatter(stacked[2], 'dp', scatter_dimension=1, tiled=True)  173 us
    reduce_scatter x1, waiting for transfers between devices, shards(): lax.psum_scatter(stacked[0], 'dp', scatter_dimension=1, tiled=True)  155 us
    psum x1, blocking collectives, shards(): lax.psum((jnp.stack(qv_parts), jnp.stack(upb_parts)), 'dp')  81.1 us
    reduce_scatter x4, waiting for transfers between devices, reduce_branch(): lax.psum_scatter(partial_term(jnp.int32(0), local_rows * lax.axis_size('t...  40.9 us
    psum x1, blocking collectives, shards(): lax.psum((jnp.stack(gain_parts), jnp.stack(shift_parts), jnp.stack(outb_p...  39.6 us
    convert_element_type x2, other arithmetic, shards(): hidden = gelu_exact(hidden_pre).astype(jnp.bfloat16)  31.1 us
    unnamed x171, local copies, waits for them, and re-layouts  25.6 us
  transfers between devices with their start and end apart: 15, of which 13 were waited for; matrix products, arithmetic and copies ran while one was open for 11% of the time, Pallas kernels for 0%

profile of v1, /device:TPU:0, one launch (start us, length us, event | category | flops | bytes accessed | tf_op | source)
XLA Modules:
  0.0 1101.7 jit_solution(16342942065898907013)
XLA Ops:
  13.2 5.3 all_to_all.20
  37.6 11.8 %reduce-scatter.11.cloned.1.call-done = bf16[2,256,768]{2,1,0:T(8,128)(2,1)} async-done(((bf16[4,256,768]{2,1,0:T(8,128)(2,1)}), bf16[2,256,768]{2,1,0:T(8,128)(2,1)}) %reduce-scatter.11.cloned.1.call-update) | async-done | bytes 786448 | tf_op jit(solution)/shard_map/reduce_scatter | solution.py:41
  53.3 5.5 all_to_all.21
  62.9 15.5 %multiply_convert_fusion.3 = (bf16[4,256,1536]{2,1,0:T(8,128)(2,1)S(1)}, f32[4,256,1536]{2,1,0:T(8,128)}) fusion(f32[4,256,1536]{2,1,0:T(8,128)S(1)} %get-tuple-element.122, f32[1536]{0:T(1024)S(1)} %get-tuple-element.73, u8[256,1536]{1,0:T(8,128)(4,1)S(1)} %get-tuple-element.51, u8[256,1536]{1,0:T(8,128)(4,1)S(1)} %get-tuple-element.50), kind=kLoop, calls=%fused_computation.40 | loop fusion | flops 111673344 | bytes 16521216 | tf_op jit(solution)/shard_map/convert_element_type | solution.py:157
  83.8 10.2 reduce-scatter.13.cloned.1.call-done
  96.7 5.7 all_to_all.22
  126.5 9.8 reduce-scatter.15.cloned.1.call-done
  139.5 5.2 all_to_all.23
  151.4 15.6 %multiply_convert_fusion.2 = (bf16[4,256,1536]{2,1,0:T(8,128)(2,1)}, f32[4,256,1536]{2,1,0:T(8,128)}) fusion(f32[4,256,1536]{2,1,0:T(8,128)S(1)} %get-tuple-element.125, f32[1536]{0:T(1024)S(1)} %get-tuple-element.72, u8[256,1536]{1,0:T(8,128)(4,1)S(1)} %get-tuple-element.49, u8[256,1536]{1,0:T(8,128)(4,1)S(1)} %get-tuple-element.48), kind=kLoop, calls=%fused_computation.24 | loop fusion | flops 111673344 | bytes 16521216 | tf_op jit(solution)/shard_map/convert_element_type | solution.py:157
  167.1 10.2 fusion.134
  179.0 5.4 fusion.68
  184.4 6.4 fusion.71
  198.1 9.1 reduce-scatter.17.cloned.1.call-done
  229.7 8.0 multiply_reduce_fusion.1
  263.3 5.6 convolution_convert_fusion.3
  269.4 9.9 reduce-scatter.21.cloned.1.call-done
  284.9 11.1 %all-gather.9.cloned.1.call-done = bf16[4,256,768]{2,1,0:T(8,128)(2,1)} async-done(((bf16[2,256,768]{2,1,0:T(8,128)(2,1)}), bf16[4,256,768]{2,1,0:T(8,128)(2,1)}) %all-gather.9.cloned.1.call-update) | async-done | bytes 1572880 | tf_op jit(solution)/shard_map/all_gather | solution.py:33
  296.0 10.2 fusion.135
  308.0 5.5 fusion.62
  313.5 10.3 reduce-scatter.23.cloned.1.call-done
  333.7 8.7 all-gather.11.cloned.1.call-done
  348.2 5.4 multiply_reduce_fusion
  374.7 5.8 convolution_convert_fusion.2
  380.7 4.8 convolution_bitcast_fusion
  395.1 15.0 %copy.141 = f32[2,1536,768]{1,0,2:T(2,128)} copy(f32[2,1536,768]{2,1,0:T(8,128)} %pad_maximum_fusion.1) | data formatting | bytes 18874368 | tf_op jit(solution)/shard_map/stack | solution.py:260
  413.9 5.3 copy.136
  419.6 5.2 convolution_bitcast_fusion.2
  450.1 81.1 %all-reduce.3 = (f32[2,2,384]{2,1,0:T(2,128)}, f32[2,1536]{1,0:T(2,128)}) all-reduce(f32[2,2,384]{2,1,0:T(2,128)S(1)} %pad_maximum_fusion.14, f32[2,1536]{1,0:T(2,128)S(1)} %pad_maximum_fusion.13), channel_id=1, replica_groups=mesh['dp'=16,'tensor'=2] {'dp'}, use_global_device_ids=true, to_apply=%region_46.47 | all-reduce | flops 4608 | bytes 36864 | tf_op jit(solution)/shard_map/psum | solution.py:270
  535.2 39.6 %all-reduce.2 = (f32[2,2,768]{2,1,0:T(2,128)}, f32[2,2,768]{2,1,0:T(2,128)}, f32[2,2,768]{2,1,0:T(2,128)}) all-reduce(f32[2,2,768]{2,1,0:T(2,128)S(1)} %pad_maximum_fusion.10, f32[2,2,768]{2,1,0:T(2,128)S(1)} %pad_maximum_fusion.11, f32[2,2,768]{2,1,0:T(2,128)S(1)} %pad_maximum_fusion.12), channel_id=1, replica_groups=mesh['dp'=16,'tensor'=2] {'dp','tensor'}, use_global_device_ids=true, to_apply=%region_35.36 | all-reduce | flops 9216 | bytes 73728 | tf_op jit(solution)/shard_map/psum | solution.py:271
  577.6 184.9 %all-reduce.7.cloned.1.call-done = (f32[2,384,768]{1,0,2:T(2,128)}, f32[2,1536,768]{1,0,2:T(2,128)}) async-done(((f32[2,384,768]{1,0,2:T(2,128)}, f32[2,1536,768]{1,0,2:T(2,128)}), (f32[2,384,768]{1,0,2:T(2,128)}, f32[2,1536,768]{1,0,2:T(2,128)})) %all-reduce.7.cloned.1.call-update) | async-done | bytes 11796496
  766.1 173.4 %reduce-scatter.29.cloned.1.call-done = f32[2,48,1536]{2,1,0:T(8,128)} async-done(((f32[2,768,1536]{2,1,0:T(8,128)}), f32[2,48,1536]{2,1,0:T(8,128)}) %reduce-scatter.29.cloned.1.call-update) | async-done | bytes 589840 | tf_op jit(solution)/shard_map/reduce_scatter | solution.py:267
  939.5 155.1 %reduce-scatter.27.cloned.1.call-done = f32[2,48,3,384]{3,1,2,0:T(8,128)} async-done(((f32[2,768,3,384]{3,1,2,0:T(8,128)}), f32[2,48,3,384]{3,1,2,0:T(8,128)}) %reduce-scatter.27.cloned.1.call-update) | async-done | bytes 442384 | tf_op jit(solution)/shard_map/reduce_scatter | solution.py:265
  (364 shorter events, 225.1 us)
Async XLA Ops:
  7.2 42.2 %reduce-scatter.11.cloned.1.call-start = ((), (), s32[]{:S(2)}) async-start(), calls=%async_computation.14 | async-start | bytes 2359296 | tf_op jit(solution)/shard_map/reduce_scatter | solution.py:41
  35.2 14.1 %copy-start.2 = (bf16[2,256,768]{2,1,0:T(8,128)(2,1)S(1)}, bf16[2,256,768]{2,1,0:T(8,128)(2,1)}, u32[]{:S(2)}) copy-start(bf16[2,256,768]{2,1,0:T(8,128)(2,1)} %param.12) | copy-start | bytes 2359300
  37.4 56.6 %reduce-scatter.13.cloned.1.call-start = ((), (), s32[]{:S(2)}) async-start(), calls=%async_computation.15 | async-start | bytes 2359296 | tf_op jit(solution)/shard_map/reduce_scatter | solution.py:41
  49.3 9.4 slice-start.6
  53.3 26.7 %slice-start.4 = ((s8[4718592]{0:T(1024)(128)(4,1)}), s8[4194304]{0:T(1024)(128)(4,1)S(1)}, s32[]{:S(2)}) async-start(s8[4718592]{0:T(1024)(128)(4,1)} %bitcast.251), calls=%async_computation.33 | async-start | bytes 8388608
  58.8 21.2 %slice-start.5 = ((s8[4718592]{0:T(1024)(128)(4,1)}), s8[524288]{0:T(1024)(128)(4,1)S(1)}, s32[]{:S(2)}) async-start(s8[4718592]{0:T(1024)(128)(4,1)} %bitcast.251), calls=%async_computation.34 | async-start | bytes 1048576
  62.9 15.5 %copy-start.25 = (f32[4,256,1536]{2,1,0:T(8,128)}, f32[4,256,1536]{2,1,0:T(8,128)S(1)}, u32[]{:S(2)}) copy-start(f32[4,256,1536]{2,1,0:T(8,128)S(1)} %get-tuple-element.122) | copy-start | bytes 18874372
  83.6 52.7 %reduce-scatter.15.cloned.1.call-start = ((), (), s32[]{:S(2)}) async-start(), calls=%async_computation.16 | async-start | bytes 2359296 | tf_op jit(solution)/shard_map/reduce_scatter | solution.py:41
  125.9 41.1 %all-gather.5.cloned.1.call-start = ((), (), s32[]{:S(2)}) async-start(), calls=%async_computation.18 | async-start | bytes 2359296 | tf_op jit(solution)/shard_map/all_gather | solution.py:33
  126.5 68.3 %reduce-scatter.19.cloned.1.call-start = ((), (), s32[]{:S(2)}) async-start(), calls=%async_computation.19 | async-start | bytes 2359296 | tf_op jit(solution)/shard_map/reduce_scatter | solution.py:54
  136.3 8.3 slice-start.8
  184.4 22.8 %reduce-scatter.17.cloned.1.call-start = ((), (), s32[]{:S(2)}) async-start(), calls=%async_computation.17 | async-start | bytes 2359296 | tf_op jit(solution)/shard_map/reduce_scatter | solution.py:41
  190.8 33.1 %all-gather.7.cloned.1.call-start = ((), (), s32[]{:S(2)}) async-start(), calls=%async_computation.20 | async-start | bytes 2359296 | tf_op jit(solution)/shard_map/all_gather | solution.py:33
  212.7 66.6 %reduce-scatter.21.cloned.1.call-start = ((), (), s32[]{:S(2)}) async-start(), calls=%async_computation.21 | async-start | bytes 2359296 | tf_op jit(solution)/shard_map/reduce_scatter | solution.py:54
  229.7 8.0 slice-start.2
  229.7 8.0 slice-start.3
  268.9 27.1 %all-gather.9.cloned.1.call-start = ((), (), s32[]{:S(2)}) async-start(), calls=%async_computation.22 | async-start | bytes 2359296 | tf_op jit(solution)/shard_map/all_gather | solution.py:33
  284.8 39.0 %reduce-scatter.23.cloned.1.call-start = ((), (), s32[]{:S(2)}) async-start(), calls=%async_computation.23 | async-start | bytes 2359296 | tf_op jit(solution)/shard_map/reduce_scatter | solution.py:54
  308.0 15.9 %copy-start.6 = (bf16[2,256,768]{2,1,0:T(8,128)(2,1)S(1)}, bf16[2,256,768]{2,1,0:T(8,128)(2,1)}, u32[]{:S(2)}) copy-start(bf16[2,256,768]{2,1,0:T(8,128)(2,1)} %reduce-scatter.11.cloned.1.call-done) | copy-start | bytes 2359300
  313.5 28.8 %all-gather.11.cloned.1.call-start = ((), (), s32[]{:S(2)}) async-start(), calls=%async_computation.24 | async-start | bytes 2359296 | tf_op jit(solution)/shard_map/all_gather | solution.py:33
  331.1 200.0 %reduce-scatter.25.cloned.1.call-start = ((), (), s32[]{:S(2)}) async-start(), calls=%async_computation.25 | async-start | bytes 2359296 | tf_op jit(solution)/shard_map/reduce_scatter | solution.py:54
  342.3 11.3 %slice-start = ((s8[6291456]{0:T(1024)(128)(4,1)}), s8[2097152]{0:T(1024)(128)(4,1)S(1)}, s32[]{:S(2)}) async-start(s8[6291456]{0:T(1024)(128)(4,1)} %bitcast.213), calls=%async_computation.29 | async-start | bytes 4194304
  363.2 7.2 copy-start.38
  380.5 382.0 %all-reduce.7.cloned.1.call-start = ((), (), s32[]{:S(2)}) async-start(), calls=%async_computation.28 | async-start | bytes 23592960
  395.1 15.0 %copy-start.69 = (bf16[4,6,64,256]{3,2,1,0:T(8,128)(2,1)S(1)}, bf16[4,6,64,256]{3,2,1,0:T(8,128)(2,1)}, u32[]{:S(2)}) copy-start(bf16[4,6,64,256]{3,2,1,0:T(8,128)(2,1)} %copy-done.68) | copy-start | bytes 2359300
  419.3 520.3 %reduce-scatter.29.cloned.1.call-start = ((), (), s32[]{:S(2)}) async-start(), calls=%async_computation.27 | async-start | bytes 10027008 | tf_op jit(solution)/shard_map/reduce_scatter | solution.py:267
  432.0 662.6 %reduce-scatter.27.cloned.1.call-start = ((), (), s32[]{:S(2)}) async-start(), calls=%async_computation.26 | async-start | bytes 7520256 | tf_op jit(solution)/shard_map/reduce_scatter | solution.py:265
  446.0 85.2 %copy-start.50 = (f32[768]{0:T(1024)S(1)}, f32[768]{0:T(1024)}, u32[]{:S(2)}) copy-start(f32[768]{0:T(1024)} %copy-done.49) | copy-start | bytes 9220
  446.0 85.2 %copy-start.52 = (f32[2,256]{1,0:T(2,128)S(1)}, f32[2,256]{1,0:T(2,128)}, u32[]{:S(2)}) copy-start(f32[2,256]{1,0:T(2,128)} %copy-done.51) | copy-start | bytes 6148
  448.0 85.0 %copy-start.58 = (f32[2,256]{1,0:T(2,128)S(1)}, f32[2,256]{1,0:T(2,128)}, u32[]{:S(2)}) copy-start(f32[2,256]{1,0:T(2,128)} %copy-done.57) | copy-start | bytes 6148
  448.0 85.0 %copy-start.56 = (f32[2,256]{1,0:T(2,128)S(1)}, f32[2,256]{1,0:T(2,128)}, u32[]{:S(2)}) copy-start(f32[2,256]{1,0:T(2,128)} %copy-done.55) | copy-start | bytes 6148
  448.2 126.5 %copy-start.8 = (f32[2,256,768]{2,1,0:T(8,128)S(1)}, f32[2,256,768]{2,1,0:T(8,128)}, u32[]{:S(2)}) copy-start(f32[2,256,768]{2,1,0:T(8,128)} %copy-done.7) | copy-start | bytes 4718596
  (66 other events, 197.0 us)
Sparse Core Ops, SparseCore 0:
  37.6 11.7 reduce-scatter.10
  83.8 10.2 reduce-scatter.12
  126.0 10.2 reduce-scatter.14
  137.8 11.0 all-gather.4
  184.5 10.2 reduce-scatter.18
  196.9 10.2 reduce-scatter.16
  212.9 11.0 all-gather.6
  269.0 10.2 reduce-scatter.20
  285.0 10.9 all-gather.8
  313.6 10.2 reduce-scatter.22
  331.3 10.9 all-gather.10
  380.6 10.2 reduce-scatter.24
  419.4 343.0 all-reduce.6
  769.5 169.9 reduce-scatter.28
  945.3 149.2 reduce-scatter.26
